TPU v7x, 32 devices: a whole 2x2x4 slice. The times are simulated.
32 devices in a mesh: circ: 8 (over z, x), cell: 4 (over y, core).
Axes of the slice: x: 2, y: 2, z: 4, core: 2. Of those that a mesh axis runs over, the one named last changes fastest.
Arguments:
- flow_state: bfloat16 [35, 8, 16, 1024], P(None, 'circ', 'cell'), may hold values from -6 to 6
- time_coef: float32 [8, 16, 1024], P('circ', 'cell'), may hold values from 0.3 to 3
- axial_damp: bfloat16 [8, 16, 1024], P('circ', 'cell'), may hold values from 0.19921875 to 2
- plane_damp: bfloat16 [8, 16, 2048], P('circ', 'cell'), may hold values from 0.19921875 to 2
- periodic_damp: bfloat16 [8, 16, 64], P('circ', 'cell'), may hold values from 0.19921875 to 2
- flux_jacobian: float32 [3, 5, 5], replicated, may hold values from -2.5 to 2.5
- face_cells: int32 [2, 2048], replicated, may hold values from 0 to 1023, as said below
- periodic_cells: int32 [2, 64], replicated, may hold values from 0 to 1023, as said below
- face_map: int32 [64], replicated, may hold values from 0 to 63, each once
- wall_cells: int32 [1024], P('cell'), may hold values from 0 to 4095, as said below
- wall_normals: float32 [3, 1024], P(None, 'cell'), may hold values from -6 to 6
- pressure_weights: float32 [5], replicated, may hold values from -4 to 4
- mode_shapes: float32 [2, 8, 3, 400], replicated, may hold values from -0.00390625 to 0.00390625
Outputs:
- jacobian_image: bfloat16 [35, 8, 16, 1024], P(None, 'circ', 'cell')
- modal_forces: float32 [7, 400], replicated
Inputs may be any that keep to these rules, and one draw needn't show every extreme that they name: `face_cells`: each column names the two cells of a layer that one in-plane face joins; the two differ. `periodic_cells`: all 128 entries differ. `face_map`: each value of 0 to 63 once. `wall_cells`: an entry is the wall cell's layer within its cell block times 1024 plus its cell in the layer; entries may repeat.
All inputs are finite; a program needn't handle non-finite values.
Results may differ from a plain program's by a relative error of at most 0.0055.
Values may be sent and summed in bfloat16 or wider, within the bound.
A program may use at most 64 MiB of HBM per device.

v0:
```python
import functools
import math

import jax
import jax.numpy as jnp
import numpy as np
from jax import lax
from jax.experimental import pallas as pl
from jax.experimental.pallas import tpu as pltpu
from jax.sharding import PartitionSpec as P

NV = 5
HB = 7
F32 = jnp.float32
BF16 = jnp.bfloat16
HI = lax.Precision.HIGHEST
MESH = pl.DeviceIdType.MESH
NT = (((1,), (1,)), ((), ()))


def up_to(value, step):
    return -(-value // step) * step


def harmonic_matrix(instances):
    matrix = np.zeros((instances, instances))
    for n in range(instances):
        for m in range(instances):
            if n != m:
                matrix[n, m] = 0.5 * (-1.0) ** (n - m) / math.sin(math.pi * (n - m) / instances)
    return matrix


def near_scale(values):
    scales = 1.0 + np.arange(4096) / 4096.0
    scaled = scales[:, None] * values[None, :]
    rounded = scaled.astype(BF16).astype(np.float64)
    return float(scales[np.argmin(np.max(np.abs(rounded / scaled - 1.0), axis=1))])


def constants(layers, passages, walls_k):
    rows = HB * NV * layers
    padded = up_to(rows, 16)
    side = up_to(HB * NV, 16)
    width = padded + 2 * side
    harmonic = harmonic_matrix(HB)
    scale = near_scale(np.unique(np.abs(harmonic[harmonic != 0])))
    mix = np.zeros((padded, padded), np.float32)
    axial = np.zeros((padded, width), np.float32)
    fixed = np.zeros((3, padded, width), np.float32)
    pick = np.zeros((2 * side, padded), np.float32)
    weights = np.zeros((8, padded), np.int32)
    of_row = np.zeros((padded, NV), np.float32)
    of_column = np.zeros((NV, width), np.float32)
    for i in range(rows):
        r, a = divmod(i, layers)
        n, v = divmod(r, NV)
        of_row[i, v] = 1
        of_column[v, i] = 1
        of_column[v, padded + r] = 1
        of_column[v, padded + side + r] = 1
        weights[n, i] = v + 1
        if a == 0:
            pick[r, i] = 1
        if a == layers - 1:
            pick[side + r, i] = 1
        for w in range(NV):
            q = n * NV + w
            mix[i, q * layers + a] = 1
            axial[i, q * layers + a + 1 if a < layers - 1 else padded + q] = 1
            axial[i, q * layers + a - 1 if a > 0 else padded + side + q] = -1
        fixed[1, i, i] = -1
        fixed[1, i, i + 1 if a < layers - 1 else padded + r] = 1
        fixed[2, i, i] = -1
        fixed[2, i, i - 1 if a > 0 else padded + side + r] = 1
        for m in range(HB):
            fixed[0, i, (m * NV + v) * layers + a] = scale * harmonic[n, m]
    lanes = up_to(walls_k * passages, 128)
    modes = np.zeros((lanes, 2 * walls_k * passages), np.float32)
    for p in range(passages):
        for d in range(passages):
            angle = 2.0 * math.pi * (d * p % passages) / passages
            for k in range(walls_k):
                modes[p * walls_k + k, k * passages + d] = math.cos(angle)
                modes[p * walls_k + k, (walls_k + k) * passages + d] = -math.sin(angle)
    arrays = (
        mix,
        axial,
        fixed.reshape(3 * padded, width).astype(BF16),
        pick.astype(BF16),
        weights,
        of_row.astype(BF16),
        of_column.astype(BF16),
        modes,
    )
    return arrays, scale


def dot(a, b):
    return jnp.dot(a, b, preferred_element_type=F32)


def kernel(
    state, time_coef, axial_damp, plane_damp, periodic_damp, jac, faces, sides, face_map,
    wall_cells, normals, press_w, mode_shapes,
    mix_c, axial_c, fixed_c, pick_c, weights_c, of_row_c, of_column_c, modes_c,
    image, modal,
    extra, signed, stack, cell_out, above, below, side_out, side_next, side_prev,
    forces_1, forces_2, flux, total,
    cell_send, cell_recv, side_send, side_recv, f1_send, f1_recv, f2_send, f2_recv,
    *, n_cell, n_circ, layers, padded, scale,
):
    me_cell = lax.axis_index("cell")
    me_circ = lax.axis_index("circ")

    def cell_at(j):
        return {"cell": lax.rem(me_cell + j, n_cell)}

    def circ_at(j):
        return {"circ": lax.rem(me_circ + j, n_circ)}

    barrier = pltpu.get_barrier_semaphore()
    for j in range(1, n_cell):
        pl.semaphore_signal(barrier, inc=1, device_id=cell_at(j), device_id_type=MESH)
    for j in range(1, n_circ):
        pl.semaphore_signal(barrier, inc=1, device_id=circ_at(j), device_id_type=MESH)

    n_rows, _, cells = state.shape
    n_faces = faces.shape[1]
    n_walls = wall_cells.shape[1]
    per = sides.shape[1]
    side_rows = above.shape[0]
    walls_k = normals.shape[0]
    groups = padded // 8

    def by_layer(value, pattern):
        return (value.reshape(groups, 8, value.shape[1]) * pattern[None]).reshape(value.shape)

    def pattern_of(rows):
        return jnp.concatenate([rows] * (8 // layers), axis=0)

    wide = state[...].astype(F32)
    pieces = [wide[r] for r in range(n_rows)]
    pieces.append(jnp.zeros((padded - n_rows * layers, cells), F32))
    u = jnp.concatenate(pieces, axis=0).astype(BF16)

    order = face_map[...]
    hits = (lax.broadcasted_iota(jnp.int32, (per, per), 0) == order).astype(F32)
    targets = jnp.dot(sides[0:1, :].astype(F32), hits, precision=HI, preferred_element_type=F32)
    targets = (targets + 0.5).astype(jnp.int32)
    wall_index = wall_cells[...]
    wall_layer = lax.div(wall_index, cells)
    wall_column = wall_index - wall_layer * cells
    columns = jnp.concatenate([wall_column, sides[1:2, :], targets], axis=1)
    high = min(256, cells)
    piece = 32
    bands = [
        (lax.broadcasted_iota(jnp.int32, (piece, 128), 0) + start).astype(F32).astype(BF16)
        for start in range(0, high, piece)
    ]
    one = jnp.ones((piece, 128), BF16)
    zero = jnp.zeros((piece, 128), BF16)

    def places(row, low):
        place = jnp.clip(row - low, -1, high).astype(F32).astype(BF16)
        return jnp.broadcast_to(place, (piece, 128))

    for at in range(extra.shape[0]):
        row = columns[:, at * 128 : (at + 1) * 128]
        for low in range(0, cells, high):
            place = places(row, low)
            for k, band in enumerate(bands):
                start = low + k * piece
                extra[at, start : start + piece, :] = jnp.where(band == place, one, zero)

    def tiles(table, first, count):
        found = [table[first // 128 + k] for k in range(count // 128)]
        return jnp.concatenate(found, axis=1)

    cell_out[0 : 2 * side_rows, :] = dot(pick_c[...], u).astype(BF16)
    damp = axial_damp[0].astype(F32)
    last = damp[layers - 1 : layers]
    cell_out[2 * side_rows :, :] = jnp.broadcast_to(last, (16, cells)).astype(BF16)

    gathered = dot(u, tiles(extra, 0, n_walls + 2 * per))
    own_side = gathered[:, n_walls:]
    side_out[0:padded, :] = own_side.astype(BF16)
    side_damp = periodic_damp[0].astype(F32)
    side_pattern = pattern_of(jnp.concatenate([side_damp, side_damp], axis=1))
    side_out[padded:, :] = jnp.concatenate([side_pattern, side_pattern], axis=0).astype(BF16)

    layer_of = lax.rem(lax.broadcasted_iota(jnp.int32, (8, n_walls), 0), layers)
    here = by_layer(gathered[:, :n_walls], (layer_of == wall_layer).astype(F32))
    weight_class = weights_c[...]
    weight = jnp.zeros(weight_class.shape, F32)
    for v in range(NV):
        weight = jnp.where(weight_class == v + 1, press_w[v], weight)
    pressure = jnp.dot(weight, here, precision=HI, preferred_element_type=F32)
    force = lax.dot_general(pressure, normals[...], NT, precision=HI, preferred_element_type=F32)
    lanes = forces_1.shape[2]
    lane = lax.broadcasted_iota(jnp.int32, (8, lanes), 1)
    tile = jnp.zeros((8, lanes), F32)
    for k in range(walls_k):
        tile = jnp.where(lane == me_circ * walls_k + k, force[:, k : k + 1], tile)
    forces_1[me_cell] = tile

    def mixing(face, mask):
        values = (0.5 * jac[:, face, :]).astype(BF16)
        across = dot(values, of_column_c[:, : mask.shape[1]]).astype(BF16)
        return (dot(of_row_c[...], across) * mask).astype(BF16)

    axial_mix = mixing(0, axial_c[...])
    plane_mix = mixing(1, mix_c[...])
    side_mix = mixing(2, mix_c[...])

    convected = dot(plane_mix, u).astype(BF16)
    plane_pattern = pattern_of(0.5 * plane_damp[0].astype(F32))

    def build(first, count):
        for at in range(first, first + count, 128):
            rows = [faces[side : side + 1, at : at + 128] for side in range(2)]
            for low in range(0, cells, high):
                owner, other = places(rows[0], low), places(rows[1], low)
                for k, band in enumerate(bands):
                    start = low + k * piece
                    hit = jnp.where(band == owner, one, jnp.where(band == other, -one, zero))
                    signed[at // 128, start : start + piece, :] = hit

    def gather(first, count):
        here = slice(first, first + count)
        table = tiles(signed, first, count)
        damped = by_layer(dot(u, table), plane_pattern[:, here])
        flux[:, here] = (dot(convected, jnp.abs(table)) + damped).astype(BF16)

    part = 256
    starts = list(range(0, n_faces, part))
    early = len(starts) // 4
    build(0, part)
    for at in starts[:early]:
        build(at + part, part)
        gather(at, part)

    pl.semaphore_wait(barrier, n_cell - 1 + n_circ - 1)
    copies = []

    def send(source, target, send_sem, recv_sem, device):
        copy = pltpu.make_async_remote_copy(
            src_ref=source, dst_ref=target, send_sem=send_sem, recv_sem=recv_sem,
            device_id=device, device_id_type=MESH,
        )
        copy.start()
        copies.append(copy)
        return copy

    to_below = send(
        cell_out.at[pl.ds(0, side_rows)], above, cell_send.at[0], cell_recv.at[0],
        cell_at(n_cell - 1),
    )
    to_above = send(
        cell_out.at[pl.ds(side_rows, side_rows + 16)], below, cell_send.at[1], cell_recv.at[1],
        cell_at(1),
    )
    to_prev = send(side_out, side_next, side_send.at[0], side_recv.at[0], circ_at(n_circ - 1))
    to_next = send(side_out, side_prev, side_send.at[1], side_recv.at[1], circ_at(1))
    first = [
        send(forces_1.at[me_cell], forces_1.at[me_cell], f1_send.at[j], f1_recv.at[j], cell_at(j))
        for j in range(1, n_cell)
    ]

    def chunks(some):
        for at in some:
            if at + part < n_faces:
                build(at + part, part)
            gather(at, part)

    joined = len(starts) // 2
    chunks(starts[early:joined])
    for copy in first:
        copy.wait_recv()
    summed = forces_1[0]
    for j in range(1, n_cell):
        summed = summed + forces_1[j]
    forces_2[0] = summed
    chunks(starts[joined : joined + 1])
    second = [
        send(forces_2.at[0], forces_2.at[j], f2_send.at[j], f2_recv.at[j], circ_at(j))
        for j in range(1, n_circ)
    ]
    chunks(starts[joined + 1 :])
    shapes = mode_shapes[...].reshape(2 * walls_k * n_circ, mode_shapes.shape[3])
    by_passage = jnp.dot(modes_c[...], shapes, precision=HI, preferred_element_type=F32)

    total[...] = lax.dot_general(
        flux[...], tiles(signed, 0, n_faces), NT, preferred_element_type=F32
    )

    to_below.wait_recv()
    to_above.wait_recv()
    stack[0:padded, :] = u
    above_rows = above[...].astype(F32)
    stack[padded : padded + side_rows, :] = jnp.where(
        me_cell == n_cell - 1, 0.0, above_rows
    ).astype(BF16)
    below_rows = below[0:side_rows, :].astype(F32)
    stack[padded + side_rows :, :] = jnp.where(
        me_cell == 0, -cell_out[0:side_rows, :].astype(F32), below_rows
    ).astype(BF16)
    below_damp = below[side_rows : side_rows + 16, :].astype(F32)[0:1]
    below_damp = jnp.where(me_cell == 0, 0.0, below_damp)
    held = stack[...]
    derived = dot(fixed_c[...], held)
    result = by_layer(derived[0:padded], pattern_of(time_coef[0] * (1.0 / scale)))
    result = result - by_layer(derived[padded : 2 * padded], pattern_of(0.5 * damp))
    lower_damp = jnp.concatenate([below_damp, damp[0 : layers - 1]], axis=0)
    result = result - by_layer(derived[2 * padded :], pattern_of(0.5 * lower_damp))
    result = result + dot(axial_mix, held)

    to_prev.wait_recv()
    to_next.wait_recv()
    left = lax.broadcasted_iota(jnp.int32, (padded, 2 * per), 1) < per
    ahead = pltpu.roll(side_next[0:padded, :].astype(F32), per, 1)
    back = pltpu.roll(side_prev[0:padded, :].astype(F32), per, 1)
    back_damp = side_prev[padded:, :].astype(F32)[0:8]
    lower = jnp.where(left, own_side, back)
    upper = jnp.where(left, ahead, own_side)
    side_s = 0.5 * jnp.where(left[0:8], side_pattern, back_damp)
    lower_b, upper_b = lower.astype(BF16), upper.astype(BF16)
    side_flux = dot(side_mix, lower_b) + dot(side_mix, upper_b)
    side_flux = side_flux - by_layer(upper - lower, side_s)
    side_flux = jnp.where(left, side_flux, -side_flux).astype(BF16)
    result = result + lax.dot_general(
        side_flux, tiles(extra, n_walls, 2 * per), NT, preferred_element_type=F32
    )
    result = result + total[...]
    for r in range(n_rows):
        image[r] = result[r * layers : (r + 1) * layers].astype(BF16)

    for copy in second:
        copy.wait_recv()
    every = forces_2[0]
    for j in range(1, n_circ):
        every = every + forces_2[j]
    answer = jnp.dot(every, by_passage, precision=HI, preferred_element_type=F32)
    modal[...] = answer[0:HB]
    for copy in copies:
        copy.wait_send()


def deliver(image, modal, image_out, modal_out, sems):
    copies = [
        pltpu.make_async_copy(image, image_out, sems.at[0]),
        pltpu.make_async_copy(modal, modal_out, sems.at[1]),
    ]
    for copy in copies:
        copy.start()
    for copy in copies:
        copy.wait()


def shards(
    flow_state, time_coef, axial_damp, plane_damp, periodic_damp, flux_jacobian, face_cells,
    periodic_cells, face_map, wall_cells, wall_normals, pressure_weights, mode_shapes,
):
    layers, cells = flow_state.shape[2:]
    n_cell = lax.axis_size("cell")
    n_circ = lax.axis_size("circ")
    walls_k = wall_normals.shape[0]
    n_modes = mode_shapes.shape[3]
    per = face_map.shape[0]
    n_faces = face_cells.shape[1]
    n_walls = wall_cells.shape[0]
    fixed, scale = constants(layers, n_circ, walls_k)
    padded = fixed[0].shape[0]
    side = fixed[3].shape[0] // 2
    lanes = fixed[7].shape[0]
    state = flow_state.reshape(HB * NV, layers, cells)
    vmem = pl.BlockSpec(memory_space=pltpu.VMEM)
    smem = pl.BlockSpec(memory_space=pltpu.SMEM)
    dma = pltpu.SemaphoreType.DMA
    image, modal = pl.pallas_call(
        functools.partial(
            kernel, n_cell=n_cell, n_circ=n_circ, layers=layers, padded=padded, scale=scale
        ),
        out_shape=(
            jax.ShapeDtypeStruct((HB * NV, layers, cells), BF16),
            jax.ShapeDtypeStruct((HB, n_modes), F32),
        ),
        in_specs=[vmem] * 11 + [smem] + [vmem] * 9,
        out_specs=(vmem, vmem),
        scratch_shapes=[
            pltpu.VMEM(((n_walls + 2 * per) // 128, cells, 128), BF16),
            pltpu.VMEM((n_faces // 128, cells, 128), BF16),
            pltpu.VMEM((padded + 2 * side, cells), BF16),
            pltpu.VMEM((2 * side + 16, cells), BF16),
            pltpu.VMEM((side, cells), BF16),
            pltpu.VMEM((side + 16, cells), BF16),
            pltpu.VMEM((padded + 16, 2 * per), BF16),
            pltpu.VMEM((padded + 16, 2 * per), BF16),
            pltpu.VMEM((padded + 16, 2 * per), BF16),
            pltpu.VMEM((n_cell, 8, lanes), F32),
            pltpu.VMEM((n_circ, 8, lanes), F32),
            pltpu.VMEM((padded, n_faces), BF16),
            pltpu.VMEM((padded, cells), F32),
            dma((2,)), dma((2,)), dma((2,)), dma((2,)),
            dma((n_cell,)), dma((n_cell,)), dma((n_circ,)), dma((n_circ,)),
        ],
        compiler_params=pltpu.CompilerParams(collective_id=0, has_side_effects=True),
    )(
        state, time_coef, axial_damp, plane_damp, periodic_damp,
        flux_jacobian.transpose(1, 0, 2), face_cells, periodic_cells, face_map[None], wall_cells[None], wall_normals, pressure_weights,
        mode_shapes.transpose(0, 2, 1, 3), *fixed,
    )
    anywhere = pl.BlockSpec(memory_space=pl.ANY)
    image, modal = pl.pallas_call(
        deliver,
        out_shape=(
            jax.ShapeDtypeStruct(image.shape, BF16),
            jax.ShapeDtypeStruct(modal.shape, F32),
        ),
        in_specs=[anywhere] * 2,
        out_specs=(vmem, vmem),
        scratch_shapes=[dma((2,))],
    )(image, modal)
    return image.reshape(HB * NV, 1, layers, cells), modal


def solution(mesh):
    circ = P("circ", "cell", None)
    placed = (
        P(None, "circ", "cell", None), circ, circ, circ, circ, P(), P(), P(), P(),
        P("cell"), P(None, "cell"), P(), P(),
    )
    return jax.shard_map(
        shards,
        mesh=mesh,
        in_specs=placed,
        out_specs=(P(None, "circ", "cell", None), P()),
        check_vma=False,
    )
```

profile of v0, /device:TPU:0, one launch (start us, length us, event | category | flops | bytes accessed | tf_op | source)
XLA Modules:
  0.0 19.5 jit_solution(9068776985462002788)
XLA Ops:
  0.6 17.1 %shard_map.212 = (bf16[35,4,1024]{2,1,0:T(4,128)(2,1)}, f32[7,400]{1,0:T(8,128)}) custom-call(bf16[35,4,1024]{2,1,0:T(4,128)(2,1)} %bitcast.8, f32[1,4,1024]{2,1,0:T(4,128)} %time_coef.1, bf16[1,4,1024]{2,1,0:T(4,128)(2,1)} %axial_damp.1, bf16[1,4,2048]{2,1,0:T(4,128)(2,1)} %plane_damp.1, bf16[1,4,64]{2,1,0:T(4,128)(2,1)} %periodic_damp.1, ...), custom_call_target="tpu_custom_call" | custom-call | tf_op jit(solution)/shard_map/pallas_call | solution.py:380
  17.8 1.7 %shard_map.213 = (bf16[35,4,1024]{2,1,0:T(4,128)(2,1)}, f32[7,400]{1,0:T(8,128)}) custom-call(bf16[35,4,1024]{2,1,0:T(4,128)(2,1)} %get-tuple-element.6.image, f32[7,400]{1,0:T(8,128)} %get-tuple-element.7.modal), custom_call_target="tpu_custom_call" | custom-call | tf_op jit(solution)/shard_map/pallas_call | solution.py:414
where the time goes:
time: 19.6 us; the launch traced here: 19.5 us
  Pallas kernels  18.8 us (96%)
  between operations  0.64 us (3%)
    pallas_call x1, Pallas kernels, shards(): pl.pallas_call(functools.partial(kernel, n_cell=n_cell, n_circ=n_circ, la...  17.1 us
    pallas_call x1, Pallas kernels, shards(): pl.pallas_call(deliver, out_shape=(jax.ShapeDtypeStruct(image.shape, BF16...  1.69 us

commit v1 on v0

--- a/solution.py
+++ b/solution.py
@@ -13,6 +13,8 @@
 HB = 7
 F32 = jnp.float32
 BF16 = jnp.bfloat16
+F8 = jnp.float8_e4m3fn
+GROUP = 32
 HI = lax.Precision.HIGHEST
 MESH = pl.DeviceIdType.MESH
 NT = (((1,), (1,)), ((), ()))
@@ -105,7 +107,7 @@
     wall_cells, normals, press_w, mode_shapes,
     mix_c, axial_c, fixed_c, pick_c, weights_c, of_row_c, of_column_c, modes_c,
     image, modal,
-    extra, signed, stack, cell_out, above, below, side_out, side_next, side_prev,
+    extra, signed, joint, stack, cell_out, above, below, side_out, side_next, side_prev,
     forces_1, forces_2, flux, total,
     cell_send, cell_recv, side_send, side_recv, f1_send, f1_recv, f2_send, f2_recv,
     *, n_cell, n_circ, layers, padded, scale,
@@ -152,37 +154,29 @@
     wall_layer = lax.div(wall_index, cells)
     wall_column = wall_index - wall_layer * cells
     columns = jnp.concatenate([wall_column, sides[1:2, :], targets], axis=1)
-    high = min(256, cells)
-    piece = 32
-    bands = [
-        (lax.broadcasted_iota(jnp.int32, (piece, 128), 0) + start).astype(F32).astype(BF16)
-        for start in range(0, high, piece)
-    ]
-    one = jnp.ones((piece, 128), BF16)
-    zero = jnp.zeros((piece, 128), BF16)
-
-    def places(row, low):
-        place = jnp.clip(row - low, -1, high).astype(F32).astype(BF16)
-        return jnp.broadcast_to(place, (piece, 128))
-
-    for at in range(extra.shape[0]):
-        row = columns[:, at * 128 : (at + 1) * 128]
-        for low in range(0, cells, high):
-            place = places(row, low)
-            for k, band in enumerate(bands):
-                start = low + k * piece
-                extra[at, start : start + piece, :] = jnp.where(band == place, one, zero)
-
-    def tiles(table, first, count):
-        found = [table[first // 128 + k] for k in range(count // 128)]
-        return jnp.concatenate(found, axis=1)
+    band = lax.broadcasted_iota(jnp.int32, (GROUP, 128), 0).astype(F32).astype(BF16)
+    one = jnp.ones((GROUP, 128), BF16)
+    zero = jnp.zeros((GROUP, 128), BF16)
+
+    def spread(row):
+        return jnp.broadcast_to(row.astype(F32).astype(BF16), (GROUP, 128))
+
+    def split(row):
+        high = lax.shift_right_logical(row, GROUP.bit_length() - 1)
+        return spread(high), jnp.where(band == spread(row - high * GROUP), one, zero)
+
+    for at in range(0, extra.shape[1], 128):
+        high, low = split(columns[:, at : at + 128])
+        for h in range(cells // GROUP):
+            hit = jnp.where(high == h, low, zero)
+            extra[h * GROUP : (h + 1) * GROUP, at : at + 128] = hit.astype(F8)
 
     cell_out[0 : 2 * side_rows, :] = dot(pick_c[...], u).astype(BF16)
     damp = axial_damp[0].astype(F32)
     last = damp[layers - 1 : layers]
     cell_out[2 * side_rows :, :] = jnp.broadcast_to(last, (16, cells)).astype(BF16)
 
-    gathered = dot(u, tiles(extra, 0, n_walls + 2 * per))
+    gathered = dot(u, extra[...])
     own_side = gathered[:, n_walls:]
     side_out[0:padded, :] = own_side.astype(BF16)
     side_damp = periodic_damp[0].astype(F32)
@@ -218,19 +212,23 @@
 
     def build(first, count):
         for at in range(first, first + count, 128):
-            rows = [faces[side : side + 1, at : at + 128] for side in range(2)]
-            for low in range(0, cells, high):
-                owner, other = places(rows[0], low), places(rows[1], low)
-                for k, band in enumerate(bands):
-                    start = low + k * piece
-                    hit = jnp.where(band == owner, one, jnp.where(band == other, -one, zero))
-                    signed[at // 128, start : start + piece, :] = hit
+            owner_high, owner = split(faces[0:1, at : at + 128])
+            other_high, other = split(faces[1:2, at : at + 128])
+            same = owner_high == other_high
+            both = owner - other
+            by_owner = jnp.where(same, both, owner)
+            by_other = jnp.where(same, both, -other)
+            for h in range(cells // GROUP):
+                hit = jnp.where(other_high == h, by_other, zero)
+                hit = jnp.where(owner_high == h, by_owner, hit)
+                here = slice(h * GROUP, (h + 1) * GROUP)
+                signed[here, at : at + 128] = hit.astype(F8)
+                joint[here, at : at + 128] = jnp.abs(hit).astype(F8)
 
     def gather(first, count):
         here = slice(first, first + count)
-        table = tiles(signed, first, count)
-        damped = by_layer(dot(u, table), plane_pattern[:, here])
-        flux[:, here] = (dot(convected, jnp.abs(table)) + damped).astype(BF16)
+        damped = by_layer(dot(u, signed[:, here]), plane_pattern[:, here])
+        flux[:, here] = (dot(convected, joint[:, here]) + damped).astype(BF16)
 
     part = 256
     starts = list(range(0, n_faces, part))
@@ -291,7 +289,7 @@
     by_passage = jnp.dot(modes_c[...], shapes, precision=HI, preferred_element_type=F32)
 
     total[...] = lax.dot_general(
-        flux[...], tiles(signed, 0, n_faces), NT, preferred_element_type=F32
+        flux[...], signed[...], NT, preferred_element_type=F32
     )
 
     to_below.wait_recv()
@@ -329,7 +327,7 @@
     side_flux = side_flux - by_layer(upper - lower, side_s)
     side_flux = jnp.where(left, side_flux, -side_flux).astype(BF16)
     result = result + lax.dot_general(
-        side_flux, tiles(extra, n_walls, 2 * per), NT, preferred_element_type=F32
+        side_flux, extra[:, n_walls:], NT, preferred_element_type=F32
     )
     result = result + total[...]
     for r in range(n_rows):
@@ -388,8 +386,9 @@
         in_specs=[vmem] * 11 + [smem] + [vmem] * 9,
         out_specs=(vmem, vmem),
         scratch_shapes=[
-            pltpu.VMEM(((n_walls + 2 * per) // 128, cells, 128), BF16),
-            pltpu.VMEM((n_faces // 128, cells, 128), BF16),
+            pltpu.VMEM((cells, n_walls + 2 * per), F8),
+            pltpu.VMEM((cells, n_faces), F8),
+            pltpu.VMEM((cells, n_faces), F8),
             pltpu.VMEM((padded + 2 * side, cells), BF16),
             pltpu.VMEM((2 * side + 16, cells), BF16),
             pltpu.VMEM((side, cells), BF16),

time: 19.6 us -> 19.5 us (level)
  no operation moved by 1% of the time
where the time goes in v1:
time: 19.5 us; the launch traced here: 19.3 us
  Pallas kernels  18.7 us (96%)
  between operations  0.64 us (3%)
    pallas_call x1, Pallas kernels, shards(): pl.pallas_call(functools.partial(kernel, n_cell=n_cell, n_circ=n_circ, la...  17 us
    pallas_call x1, Pallas kernels, shards(): pl.pallas_call(deliver, out_shape=(jax.ShapeDtypeStruct(image.shape, BF16...  1.69 us

profile of v1, /device:TPU:0, one launch (start us, length us, event | category | flops | bytes accessed | tf_op | source)
XLA Modules:
  0.0 19.3 jit_solution(17691225276474038267)
XLA Ops:
  0.6 17.0 %shard_map.212 = (bf16[35,4,1024]{2,1,0:T(4,128)(2,1)}, f32[7,400]{1,0:T(8,128)}) custom-call(bf16[35,4,1024]{2,1,0:T(4,128)(2,1)} %bitcast.8, f32[1,4,1024]{2,1,0:T(4,128)} %time_coef.1, bf16[1,4,1024]{2,1,0:T(4,128)(2,1)} %axial_damp.1, bf16[1,4,2048]{2,1,0:T(4,128)(2,1)} %plane_damp.1, bf16[1,4,64]{2,1,0:T(4,128)(2,1)} %periodic_damp.1, ...), custom_call_target="tpu_custom_call" | custom-call | tf_op jit(solution)/shard_map/pallas_call | solution.py:378
  17.6 1.7 %shard_map.213 = (bf16[35,4,1024]{2,1,0:T(4,128)(2,1)}, f32[7,400]{1,0:T(8,128)}) custom-call(bf16[35,4,1024]{2,1,0:T(4,128)(2,1)} %get-tuple-element.6.image, f32[7,400]{1,0:T(8,128)} %get-tuple-element.7.modal), custom_call_target="tpu_custom_call" | custom-call | tf_op jit(solution)/shard_map/pallas_call | solution.py:413

commit v2 on v1

--- a/solution.py
+++ b/solution.py
@@ -15,6 +15,17 @@
 BF16 = jnp.bfloat16
 F8 = jnp.float8_e4m3fn
 GROUP = 32
+VMEM_LIMIT = 24 << 20
+(
+    STATE, TIME_COEF, AXIAL_DAMP, PLANE_DAMP, PERIODIC_DAMP, JAC, FACES, SIDES, FACE_MAP,
+    WALL_CELLS, NORMALS, PRESS_W, MODE_SHAPES,
+    MIX_C, AXIAL_C, FIXED_C, PICK_C, WEIGHTS_C, OF_ROW_C, OF_COLUMN_C, MODES_C,
+) = range(21)
+LOAD_ORDER = (
+    STATE, WALL_CELLS, NORMALS, PRESS_W, WEIGHTS_C, FACE_MAP, SIDES, PERIODIC_DAMP, AXIAL_DAMP,
+    PICK_C, JAC, OF_ROW_C, OF_COLUMN_C, MIX_C, AXIAL_C, PLANE_DAMP, FACES, MODE_SHAPES, MODES_C,
+    FIXED_C, TIME_COEF,
+)
 HI = lax.Precision.HIGHEST
 MESH = pl.DeviceIdType.MESH
 NT = (((1,), (1,)), ((), ()))
@@ -38,6 +49,12 @@
     scaled = scales[:, None] * values[None, :]
     rounded = scaled.astype(BF16).astype(np.float64)
     return float(scales[np.argmin(np.max(np.abs(rounded / scaled - 1.0), axis=1))])
+
+
+def force_slots(passages, walls_k):
+    pitch = up_to(walls_k * 8, 32)
+    per_row = 128 // pitch
+    return pitch, per_row, up_to(passages, per_row) // per_row * 128
 
 
 def constants(layers, passages, walls_k):
@@ -77,8 +94,7 @@
         fixed[2, i, i - 1 if a > 0 else padded + side + r] = 1
         for m in range(HB):
             fixed[0, i, (m * NV + v) * layers + a] = scale * harmonic[n, m]
-    lanes = up_to(walls_k * passages, 128)
-    modes = np.zeros((lanes, 2 * walls_k * passages), np.float32)
+    modes = np.zeros((up_to(walls_k * passages, 16), 2 * walls_k * passages), np.float32)
     for p in range(passages):
         for d in range(passages):
             angle = 2.0 * math.pi * (d * p % passages) / passages
@@ -86,8 +102,8 @@
                 modes[p * walls_k + k, k * passages + d] = math.cos(angle)
                 modes[p * walls_k + k, (walls_k + k) * passages + d] = -math.sin(angle)
     arrays = (
-        mix,
-        axial,
+        mix.astype(BF16),
+        axial.astype(BF16),
         fixed.reshape(3 * padded, width).astype(BF16),
         pick.astype(BF16),
         weights,
@@ -103,17 +119,24 @@
 
 
 def kernel(
-    state, time_coef, axial_damp, plane_damp, periodic_damp, jac, faces, sides, face_map,
-    wall_cells, normals, press_w, mode_shapes,
-    mix_c, axial_c, fixed_c, pick_c, weights_c, of_row_c, of_column_c, modes_c,
-    image, modal,
-    extra, signed, joint, stack, cell_out, above, below, side_out, side_next, side_prev,
-    forces_1, forces_2, flux, total,
-    cell_send, cell_recv, side_send, side_recv, f1_send, f1_recv, f2_send, f2_recv,
-    *, n_cell, n_circ, layers, padded, scale,
+    *refs, n_in, n_cell, n_circ, layers, padded, scale,
 ):
+    sources = refs[:n_in]
+    image, modal = refs[n_in : n_in + 2]
+    held_in = refs[n_in + 2 : 2 * n_in + 2]
+    (
+        state, time_coef, axial_damp, plane_damp, periodic_damp, jac, faces, sides, face_map,
+        wall_cells, normals, press_w, mode_shapes,
+        mix_c, axial_c, fixed_c, pick_c, weights_c, of_row_c, of_column_c, modes_c,
+    ) = held_in
+    (
+        extra, signed, joint, stack, cell_out, above, below, side_out, side_next, side_prev,
+        forces, modes_high, modes_low, flux, total,
+        cell_send, cell_recv, side_send, side_recv, force_send, force_recv, load_sem,
+    ) = refs[2 * n_in + 2 :]
     me_cell = lax.axis_index("cell")
     me_circ = lax.axis_index("circ")
+    me = me_circ * n_cell + me_cell
 
     def cell_at(j):
         return {"cell": lax.rem(me_cell + j, n_cell)}
@@ -121,11 +144,27 @@
     def circ_at(j):
         return {"circ": lax.rem(me_circ + j, n_circ)}
 
+    def peer(i, j):
+        return {"circ": lax.rem(me_circ + i, n_circ), "cell": lax.rem(me_cell + j, n_cell)}
+
+    peers = [(i, j) for i in range(n_circ) for j in range(n_cell) if i or j]
+    loads = {}
+
+    def fetch(which):
+        for at in which:
+            loads[at] = pltpu.make_async_copy(sources[at], held_in[at], load_sem.at[at])
+            loads[at].start()
+
+    fetch(LOAD_ORDER[:2])
+    peers = [(i, j) for i in range(n_circ) for j in range(n_cell) if i or j]
     barrier = pltpu.get_barrier_semaphore()
-    for j in range(1, n_cell):
-        pl.semaphore_signal(barrier, inc=1, device_id=cell_at(j), device_id_type=MESH)
-    for j in range(1, n_circ):
-        pl.semaphore_signal(barrier, inc=1, device_id=circ_at(j), device_id_type=MESH)
+    for i, j in peers:
+        pl.semaphore_signal(barrier, inc=1, device_id=peer(i, j), device_id_type=MESH)
+    fetch(LOAD_ORDER[2:])
+
+    def load(*which):
+        for at in which:
+            loads.pop(at).wait()
 
     n_rows, _, cells = state.shape
     n_faces = faces.shape[1]
@@ -141,67 +180,107 @@
     def pattern_of(rows):
         return jnp.concatenate([rows] * (8 // layers), axis=0)
 
+    copies = []
+
+    def send(source, target, send_sem, recv_sem, device):
+        copy = pltpu.make_async_remote_copy(
+            src_ref=source, dst_ref=target, send_sem=send_sem, recv_sem=recv_sem,
+            device_id=device, device_id_type=MESH,
+        )
+        copy.start()
+        copies.append(copy)
+        return copy
+
+    band = lax.broadcasted_iota(jnp.int32, (GROUP, 128), 0).astype(F32).astype(BF16)
+    one = jnp.ones((GROUP, 128), BF16)
+    zero = jnp.zeros((GROUP, 128), BF16)
+
+    def spread(row):
+        return jnp.broadcast_to(row.astype(F32).astype(BF16), (GROUP, 128))
+
+    def split(row):
+        high = lax.shift_right_logical(row, GROUP.bit_length() - 1)
+        return spread(high), jnp.where(band == spread(row - high * GROUP), one, zero)
+
+    def mark(columns, first):
+        for at in range(0, columns.shape[1], 128):
+            high, low = split(columns[:, at : at + 128])
+            for h in range(cells // GROUP):
+                hit = jnp.where(high == h, low, zero)
+                here = slice(first + at, first + at + 128)
+                extra[h * GROUP : (h + 1) * GROUP, here] = hit.astype(F8)
+
+    load(WALL_CELLS)
+    wall_index = wall_cells[...]
+    wall_layer = lax.div(wall_index, cells)
+    mark(wall_index - wall_layer * cells, 0)
+
+    load(STATE)
     wide = state[...].astype(F32)
     pieces = [wide[r] for r in range(n_rows)]
     pieces.append(jnp.zeros((padded - n_rows * layers, cells), F32))
     u = jnp.concatenate(pieces, axis=0).astype(BF16)
-
+    stack[0:padded, :] = u
+
+    load(NORMALS, PRESS_W, WEIGHTS_C)
+    gathered = dot(u, extra[:, 0:n_walls])
+    layer_of = lax.rem(lax.broadcasted_iota(jnp.int32, (8, n_walls), 0), layers)
+    here = by_layer(gathered, (layer_of == wall_layer).astype(F32)).astype(BF16)
+    weight_class = weights_c[...]
+    weight = jnp.zeros(weight_class.shape, F32)
+    for v in range(NV):
+        weight = jnp.where(weight_class == v + 1, press_w[v], weight)
+    high = weight.astype(BF16)
+    low = (weight - high.astype(F32)).astype(BF16)
+    pressure = dot(high, here) + dot(low, here)
+    pitch, per_row, _ = force_slots(n_circ, walls_k)
+    lane = lax.broadcasted_iota(jnp.int32, (8, 128), 1)
+    lane = lane - lax.broadcasted_iota(jnp.int32, (8, 128), 0) - lax.rem(me_circ, per_row) * pitch
+    tile = jnp.zeros((8, 128), F32)
+    for k in range(walls_k):
+        force = jnp.sum(pressure * normals[k : k + 1, :], axis=1, keepdims=True)
+        tile = jnp.where(lane == k * 8, force, tile)
+    forces[me] = jnp.sum(tile, axis=0, keepdims=True)
+
+    pl.semaphore_wait(barrier, n_cell * n_circ - 1)
+    for i, j in peers:
+        send(forces.at[me], forces.at[me], force_send, force_recv, peer(i, j))
+    copies.clear()
+
+    load(FACE_MAP, SIDES, PERIODIC_DAMP, AXIAL_DAMP, PICK_C)
     order = face_map[...]
     hits = (lax.broadcasted_iota(jnp.int32, (per, per), 0) == order).astype(F32)
     targets = jnp.dot(sides[0:1, :].astype(F32), hits, precision=HI, preferred_element_type=F32)
     targets = (targets + 0.5).astype(jnp.int32)
-    wall_index = wall_cells[...]
-    wall_layer = lax.div(wall_index, cells)
-    wall_column = wall_index - wall_layer * cells
-    columns = jnp.concatenate([wall_column, sides[1:2, :], targets], axis=1)
-    band = lax.broadcasted_iota(jnp.int32, (GROUP, 128), 0).astype(F32).astype(BF16)
-    one = jnp.ones((GROUP, 128), BF16)
-    zero = jnp.zeros((GROUP, 128), BF16)
-
-    def spread(row):
-        return jnp.broadcast_to(row.astype(F32).astype(BF16), (GROUP, 128))
-
-    def split(row):
-        high = lax.shift_right_logical(row, GROUP.bit_length() - 1)
-        return spread(high), jnp.where(band == spread(row - high * GROUP), one, zero)
-
-    for at in range(0, extra.shape[1], 128):
-        high, low = split(columns[:, at : at + 128])
-        for h in range(cells // GROUP):
-            hit = jnp.where(high == h, low, zero)
-            extra[h * GROUP : (h + 1) * GROUP, at : at + 128] = hit.astype(F8)
+    mark(jnp.concatenate([sides[1:2, :], targets], axis=1), n_walls)
 
     cell_out[0 : 2 * side_rows, :] = dot(pick_c[...], u).astype(BF16)
     damp = axial_damp[0].astype(F32)
     last = damp[layers - 1 : layers]
     cell_out[2 * side_rows :, :] = jnp.broadcast_to(last, (16, cells)).astype(BF16)
-
-    gathered = dot(u, extra[...])
-    own_side = gathered[:, n_walls:]
+    to_below = send(
+        cell_out.at[pl.ds(0, side_rows)], above, cell_send.at[0], cell_recv.at[0],
+        cell_at(n_cell - 1),
+    )
+    to_above = send(
+        cell_out.at[pl.ds(side_rows, side_rows + 16)], below, cell_send.at[1], cell_recv.at[1],
+        cell_at(1),
+    )
+
+    own_side = dot(u, extra[:, n_walls:])
     side_out[0:padded, :] = own_side.astype(BF16)
     side_damp = periodic_damp[0].astype(F32)
     side_pattern = pattern_of(jnp.concatenate([side_damp, side_damp], axis=1))
     side_out[padded:, :] = jnp.concatenate([side_pattern, side_pattern], axis=0).astype(BF16)
-
-    layer_of = lax.rem(lax.broadcasted_iota(jnp.int32, (8, n_walls), 0), layers)
-    here = by_layer(gathered[:, :n_walls], (layer_of == wall_layer).astype(F32))
-    weight_class = weights_c[...]
-    weight = jnp.zeros(weight_class.shape, F32)
-    for v in range(NV):
-        weight = jnp.where(weight_class == v + 1, press_w[v], weight)
-    pressure = jnp.dot(weight, here, precision=HI, preferred_element_type=F32)
-    force = lax.dot_general(pressure, normals[...], NT, precision=HI, preferred_element_type=F32)
-    lanes = forces_1.shape[2]
-    lane = lax.broadcasted_iota(jnp.int32, (8, lanes), 1)
-    tile = jnp.zeros((8, lanes), F32)
-    for k in range(walls_k):
-        tile = jnp.where(lane == me_circ * walls_k + k, force[:, k : k + 1], tile)
-    forces_1[me_cell] = tile
+    to_prev = send(side_out, side_next, side_send.at[0], side_recv.at[0], circ_at(n_circ - 1))
+    to_next = send(side_out, side_prev, side_send.at[1], side_recv.at[1], circ_at(1))
+
+    load(JAC, OF_ROW_C, OF_COLUMN_C, MIX_C, AXIAL_C, PLANE_DAMP, FACES)
 
     def mixing(face, mask):
         values = (0.5 * jac[:, face, :]).astype(BF16)
         across = dot(values, of_column_c[:, : mask.shape[1]]).astype(BF16)
-        return (dot(of_row_c[...], across) * mask).astype(BF16)
+        return (dot(of_row_c[...], across) * mask.astype(F32)).astype(BF16)
 
     axial_mix = mixing(0, axial_c[...])
     plane_mix = mixing(1, mix_c[...])
@@ -232,61 +311,26 @@
 
     part = 256
     starts = list(range(0, n_faces, part))
-    early = len(starts) // 4
     build(0, part)
-    for at in starts[:early]:
-        build(at + part, part)
+    for at in starts:
+        if at + part < n_faces:
+            build(at + part, part)
         gather(at, part)
 
-    pl.semaphore_wait(barrier, n_cell - 1 + n_circ - 1)
-    copies = []
-
-    def send(source, target, send_sem, recv_sem, device):
-        copy = pltpu.make_async_remote_copy(
-            src_ref=source, dst_ref=target, send_sem=send_sem, recv_sem=recv_sem,
-            device_id=device, device_id_type=MESH,
-        )
-        copy.start()
-        copies.append(copy)
-        return copy
-
-    to_below = send(
-        cell_out.at[pl.ds(0, side_rows)], above, cell_send.at[0], cell_recv.at[0],
-        cell_at(n_cell - 1),
-    )
-    to_above = send(
-        cell_out.at[pl.ds(side_rows, side_rows + 16)], below, cell_send.at[1], cell_recv.at[1],
-        cell_at(1),
-    )
-    to_prev = send(side_out, side_next, side_send.at[0], side_recv.at[0], circ_at(n_circ - 1))
-    to_next = send(side_out, side_prev, side_send.at[1], side_recv.at[1], circ_at(1))
-    first = [
-        send(forces_1.at[me_cell], forces_1.at[me_cell], f1_send.at[j], f1_recv.at[j], cell_at(j))
-        for j in range(1, n_cell)
-    ]
-
-    def chunks(some):
-        for at in some:
-            if at + part < n_faces:
-                build(at + part, part)
-            gather(at, part)
-
-    joined = len(starts) // 2
-    chunks(starts[early:joined])
-    for copy in first:
-        copy.wait_recv()
-    summed = forces_1[0]
-    for j in range(1, n_cell):
-        summed = summed + forces_1[j]
-    forces_2[0] = summed
-    chunks(starts[joined : joined + 1])
-    second = [
-        send(forces_2.at[0], forces_2.at[j], f2_send.at[j], f2_recv.at[j], circ_at(j))
-        for j in range(1, n_circ)
-    ]
-    chunks(starts[joined + 1 :])
+    load(MODE_SHAPES, MODES_C)
     shapes = mode_shapes[...].reshape(2 * walls_k * n_circ, mode_shapes.shape[3])
     by_passage = jnp.dot(modes_c[...], shapes, precision=HI, preferred_element_type=F32)
+    modes_high[...] = jnp.zeros(modes_high.shape, BF16)
+    modes_low[...] = jnp.zeros(modes_low.shape, BF16)
+    for p in range(n_circ):
+        first = p // per_row * 128 + p % per_row * pitch
+        rows = [by_passage[p * walls_k + k : p * walls_k + k + 1] for k in range(walls_k)]
+        rows = [jnp.broadcast_to(row, (8, row.shape[1])) for row in rows]
+        rows += [jnp.zeros_like(rows[0])] * (pitch // 8 - walls_k)
+        rows = jnp.concatenate(rows, axis=0)
+        high = rows.astype(BF16)
+        modes_high[first : first + pitch, :] = high
+        modes_low[first : first + pitch, :] = (rows - high.astype(F32)).astype(BF16)
 
     total[...] = lax.dot_general(
         flux[...], signed[...], NT, preferred_element_type=F32
@@ -294,7 +338,7 @@
 
     to_below.wait_recv()
     to_above.wait_recv()
-    stack[0:padded, :] = u
+    load(FIXED_C, TIME_COEF)
     above_rows = above[...].astype(F32)
     stack[padded : padded + side_rows, :] = jnp.where(
         me_cell == n_cell - 1, 0.0, above_rows
@@ -333,13 +377,28 @@
     for r in range(n_rows):
         image[r] = result[r * layers : (r + 1) * layers].astype(BF16)
 
-    for copy in second:
-        copy.wait_recv()
-    every = forces_2[0]
-    for j in range(1, n_circ):
-        every = every + forces_2[j]
-    answer = jnp.dot(every, by_passage, precision=HI, preferred_element_type=F32)
+    others = n_cell * n_circ - 1
+    arrived = pltpu.make_async_remote_copy(
+        src_ref=forces.at[pl.ds(0, others)], dst_ref=forces.at[pl.ds(0, others)],
+        send_sem=force_send, recv_sem=force_recv, device_id=peer(0, 1), device_id_type=MESH,
+    )
+    arrived.wait_recv()
+    sublane = lax.broadcasted_iota(jnp.int32, (8, 128), 0)
+    kept = lax.rem(lax.broadcasted_iota(jnp.int32, (8, 128), 1), 8) == sublane
+    rows = []
+    for first in range(0, n_circ, per_row):
+        slots = range(first * n_cell, min(first + per_row, n_circ) * n_cell)
+        row = [forces[slot] for slot in slots]
+        while len(row) > 1:
+            row = [a + b for a, b in zip(row[::2], row[1::2])] + row[len(row) // 2 * 2 :]
+        rows.append(jnp.where(kept, jnp.broadcast_to(row[0], (8, 128)), 0.0))
+    every = jnp.concatenate(rows, axis=1)
+    high = every.astype(BF16)
+    low = (every - high.astype(F32)).astype(BF16)
+    table = modes_high[...]
+    answer = dot(high, table) + dot(low, table) + dot(high, modes_low[...])
     modal[...] = answer[0:HB]
+    arrived.wait_send()
     for copy in copies:
         copy.wait_send()
 
@@ -370,22 +429,34 @@
     fixed, scale = constants(layers, n_circ, walls_k)
     padded = fixed[0].shape[0]
     side = fixed[3].shape[0] // 2
-    lanes = fixed[7].shape[0]
+    lanes = force_slots(n_circ, walls_k)[2]
     state = flow_state.reshape(HB * NV, layers, cells)
     vmem = pl.BlockSpec(memory_space=pltpu.VMEM)
-    smem = pl.BlockSpec(memory_space=pltpu.SMEM)
     dma = pltpu.SemaphoreType.DMA
+    operands = (
+        state, time_coef, axial_damp, plane_damp, periodic_damp,
+        flux_jacobian.transpose(1, 0, 2), face_cells, periodic_cells, face_map[None],
+        wall_cells[None], wall_normals, pressure_weights,
+        mode_shapes.transpose(0, 2, 1, 3), *(jnp.asarray(array) for array in fixed),
+    )
+    hbm = pl.BlockSpec(memory_space=pltpu.HBM)
+    held = [
+        (pltpu.SMEM if at == PRESS_W else pltpu.VMEM)(array.shape, array.dtype)
+        for at, array in enumerate(operands)
+    ]
     image, modal = pl.pallas_call(
         functools.partial(
-            kernel, n_cell=n_cell, n_circ=n_circ, layers=layers, padded=padded, scale=scale
+            kernel, n_in=len(operands), n_cell=n_cell, n_circ=n_circ, layers=layers,
+            padded=padded, scale=scale,
         ),
         out_shape=(
             jax.ShapeDtypeStruct((HB * NV, layers, cells), BF16),
             jax.ShapeDtypeStruct((HB, n_modes), F32),
         ),
-        in_specs=[vmem] * 11 + [smem] + [vmem] * 9,
+        in_specs=[hbm] * len(operands),
         out_specs=(vmem, vmem),
         scratch_shapes=[
+            *held,
             pltpu.VMEM((cells, n_walls + 2 * per), F8),
             pltpu.VMEM((cells, n_faces), F8),
             pltpu.VMEM((cells, n_faces), F8),
@@ -396,29 +467,27 @@
             pltpu.VMEM((padded + 16, 2 * per), BF16),
             pltpu.VMEM((padded + 16, 2 * per), BF16),
             pltpu.VMEM((padded + 16, 2 * per), BF16),
-            pltpu.VMEM((n_cell, 8, lanes), F32),
-            pltpu.VMEM((n_circ, 8, lanes), F32),
+            pltpu.VMEM((n_circ * n_cell, 1, 128), F32),
+            pltpu.VMEM((lanes, n_modes), BF16),
+            pltpu.VMEM((lanes, n_modes), BF16),
             pltpu.VMEM((padded, n_faces), BF16),
             pltpu.VMEM((padded, cells), F32),
-            dma((2,)), dma((2,)), dma((2,)), dma((2,)),
-            dma((n_cell,)), dma((n_cell,)), dma((n_circ,)), dma((n_circ,)),
+            dma((2,)), dma((2,)), dma((2,)), dma((2,)), dma, dma, dma((len(operands),)),
         ],
-        compiler_params=pltpu.CompilerParams(collective_id=0, has_side_effects=True),
-    )(
-        state, time_coef, axial_damp, plane_damp, periodic_damp,
-        flux_jacobian.transpose(1, 0, 2), face_cells, periodic_cells, face_map[None], wall_cells[None], wall_normals, pressure_weights,
-        mode_shapes.transpose(0, 2, 1, 3), *fixed,
-    )
-    anywhere = pl.BlockSpec(memory_space=pl.ANY)
+        compiler_params=pltpu.CompilerParams(
+            collective_id=0, has_side_effects=True, vmem_limit_bytes=VMEM_LIMIT
+        ),
+    )(*(pltpu.with_memory_space_constraint(array, pltpu.HBM) for array in operands))
     image, modal = pl.pallas_call(
         deliver,
         out_shape=(
             jax.ShapeDtypeStruct(image.shape, BF16),
             jax.ShapeDtypeStruct(modal.shape, F32),
         ),
-        in_specs=[anywhere] * 2,
-        out_specs=(vmem, vmem),
+        in_specs=[vmem] * 2,
+        out_specs=(hbm, hbm),
         scratch_shapes=[dma((2,))],
+        compiler_params=pltpu.CompilerParams(vmem_limit_bytes=VMEM_LIMIT),
     )(image, modal)
     return image.reshape(HB * NV, 1, layers, cells), modal
 

time: 19.5 us -> 14.5 us (0.74)
  Pallas kernels: 18.7 us -> 13.7 us
    pallas_call x1, Pallas kernels: 17 us -> 13 us  [shards(): pl.pallas_call(functools.partial(kernel, n_in=len(operands), n_cell=n_cel...]
    pallas_call x1, Pallas kernels: 1.69 us -> 0.73 us  [shards(): pl.pallas_call(deliver, out_shape=(jax.ShapeDtypeStruct(image.shape, BF16...]
where the time goes in v2:
time: 14.5 us; the launch traced here: 14.4 us
  Pallas kernels  13.7 us (94%)
  between operations  0.64 us (4%)
    pallas_call x1, Pallas kernels, shards(): pl.pallas_call(functools.partial(kernel, n_in=len(operands), n_cell=n_cel...  13 us
    pallas_call x1, Pallas kernels, shards(): pl.pallas_call(deliver, out_shape=(jax.ShapeDtypeStruct(image.shape, BF16...  0.73 us

profile of v2, /device:TPU:0, one launch (start us, length us, event | category | flops | bytes accessed | tf_op | source)
XLA Modules:
  0.0 14.4 jit_solution(15635915602172950548)
XLA Ops:
  0.6 13.0 %shard_map.212 = (bf16[35,4,1024]{2,1,0:T(4,128)(2,1)S(1)}, f32[7,400]{1,0:T(8,128)S(1)}) custom-call(bf16[35,4,1024]{2,1,0:T(4,128)(2,1)} %bitcast.8, f32[1,4,1024]{2,1,0:T(4,128)} %refs_1_.1, bf16[1,4,1024]{2,1,0:T(4,128)(2,1)} %refs_2_.1, bf16[1,4,2048]{2,1,0:T(4,128)(2,1)} %refs_3_.1, bf16[1,4,64]{2,1,0:T(4,128)(2,1)} %refs_4_.1, f32[5,3,5]{2,1,0:T(4,128)} %bitcast.10, ...), custom_call_target="tpu_custom_call" | custom-call | tf_op jit(solution)/shard_map/pallas_call | solution.py:447
  13.6 0.7 %shard_map.213 = (bf16[35,4,1024]{2,1,0:T(4,128)(2,1)}, f32[7,400]{1,0:T(8,128)}) custom-call(bf16[35,4,1024]{2,1,0:T(4,128)(2,1)S(1)} %get-tuple-element.6.image, f32[7,400]{1,0:T(8,128)S(1)} %get-tuple-element.7.modal), custom_call_target="tpu_custom_call" | custom-call | tf_op jit(solution)/shard_map/pallas_call | solution.py:481

commit v3 on v2

--- a/solution.py
+++ b/solution.py
@@ -180,16 +180,27 @@
     def pattern_of(rows):
         return jnp.concatenate([rows] * (8 // layers), axis=0)
 
-    copies = []
-
-    def send(source, target, send_sem, recv_sem, device):
-        copy = pltpu.make_async_remote_copy(
+    def remote(source, target, send_sem, recv_sem, device):
+        return pltpu.make_async_remote_copy(
             src_ref=source, dst_ref=target, send_sem=send_sem, recv_sem=recv_sem,
             device_id=device, device_id_type=MESH,
         )
-        copy.start()
-        copies.append(copy)
-        return copy
+
+    to_below = remote(
+        cell_out.at[pl.ds(0, side_rows)], above, cell_send.at[0], cell_recv.at[0],
+        cell_at(n_cell - 1),
+    )
+    to_above = remote(
+        cell_out.at[pl.ds(side_rows, side_rows + 16)], below, cell_send.at[1], cell_recv.at[1],
+        cell_at(1),
+    )
+    to_prev = remote(side_out, side_next, side_send.at[0], side_recv.at[0], circ_at(n_circ - 1))
+    to_next = remote(side_out, side_prev, side_send.at[1], side_recv.at[1], circ_at(1))
+    copies = [to_below, to_above, to_prev, to_next]
+
+    def send_sides():
+        for copy in copies:
+            copy.start()
 
     band = lax.broadcasted_iota(jnp.int32, (GROUP, 128), 0).astype(F32).astype(BF16)
     one = jnp.ones((GROUP, 128), BF16)
@@ -242,10 +253,14 @@
         tile = jnp.where(lane == k * 8, force, tile)
     forces[me] = jnp.sum(tile, axis=0, keepdims=True)
 
-    pl.semaphore_wait(barrier, n_cell * n_circ - 1)
-    for i, j in peers:
-        send(forces.at[me], forces.at[me], force_send, force_recv, peer(i, j))
-    copies.clear()
+    late = me_circ >= n_circ // 2
+
+    def enter_and_send_forces():
+        pl.semaphore_wait(barrier, n_cell * n_circ - 1)
+        for i, j in peers:
+            remote(forces.at[me], forces.at[me], force_send, force_recv, peer(i, j)).start()
+
+    pl.when(late)(enter_and_send_forces)
 
     load(FACE_MAP, SIDES, PERIODIC_DAMP, AXIAL_DAMP, PICK_C)
     order = face_map[...]
@@ -258,22 +273,12 @@
     damp = axial_damp[0].astype(F32)
     last = damp[layers - 1 : layers]
     cell_out[2 * side_rows :, :] = jnp.broadcast_to(last, (16, cells)).astype(BF16)
-    to_below = send(
-        cell_out.at[pl.ds(0, side_rows)], above, cell_send.at[0], cell_recv.at[0],
-        cell_at(n_cell - 1),
-    )
-    to_above = send(
-        cell_out.at[pl.ds(side_rows, side_rows + 16)], below, cell_send.at[1], cell_recv.at[1],
-        cell_at(1),
-    )
-
     own_side = dot(u, extra[:, n_walls:])
     side_out[0:padded, :] = own_side.astype(BF16)
     side_damp = periodic_damp[0].astype(F32)
     side_pattern = pattern_of(jnp.concatenate([side_damp, side_damp], axis=1))
     side_out[padded:, :] = jnp.concatenate([side_pattern, side_pattern], axis=0).astype(BF16)
-    to_prev = send(side_out, side_next, side_send.at[0], side_recv.at[0], circ_at(n_circ - 1))
-    to_next = send(side_out, side_prev, side_send.at[1], side_recv.at[1], circ_at(1))
+    pl.when(late)(send_sides)
 
     load(JAC, OF_ROW_C, OF_COLUMN_C, MIX_C, AXIAL_C, PLANE_DAMP, FACES)
 
@@ -335,6 +340,11 @@
     total[...] = lax.dot_general(
         flux[...], signed[...], NT, preferred_element_type=F32
     )
+
+    @pl.when(jnp.logical_not(late))
+    def _():
+        enter_and_send_forces()
+        send_sides()
 
     to_below.wait_recv()
     to_above.wait_recv()

time: 14.5 us -> 14.2 us (0.979)
  Pallas kernels: 13.7 us -> 13.3 us
    pallas_call x1, Pallas kernels: 13 us -> 12.6 us  [shards(): pl.pallas_call(functools.partial(kernel, n_in=len(operands), n_cell=n_cel...]
where the time goes in v3:
time: 14.2 us; the launch traced here: 13.9 us
  Pallas kernels  13.3 us (94%)
  between operations  0.64 us (5%)
    pallas_call x1, Pallas kernels, shards(): pl.pallas_call(functools.partial(kernel, n_in=len(operands), n_cell=n_cel...  12.6 us
    pallas_call x1, Pallas kernels, shards(): pl.pallas_call(deliver, out_shape=(jax.ShapeDtypeStruct(image.shape, BF16...  0.73 us

profile of v3, /device:TPU:0, one launch (start us, length us, event | category | flops | bytes accessed | tf_op | source)
XLA Modules:
  0.0 13.9 jit_solution(5759880434706614217)
XLA Ops:
  0.6 12.6 %shard_map.212 = (bf16[35,4,1024]{2,1,0:T(4,128)(2,1)S(1)}, f32[7,400]{1,0:T(8,128)S(1)}) custom-call(bf16[35,4,1024]{2,1,0:T(4,128)(2,1)} %bitcast.8, f32[1,4,1024]{2,1,0:T(4,128)} %refs_1_.1, bf16[1,4,1024]{2,1,0:T(4,128)(2,1)} %refs_2_.1, bf16[1,4,2048]{2,1,0:T(4,128)(2,1)} %refs_3_.1, bf16[1,4,64]{2,1,0:T(4,128)(2,1)} %refs_4_.1, f32[5,3,5]{2,1,0:T(4,128)} %bitcast.10, ...), custom_call_target="tpu_custom_call" | custom-call | tf_op jit(solution)/shard_map/pallas_call | solution.py:457
  13.2 0.7 %shard_map.213 = (bf16[35,4,1024]{2,1,0:T(4,128)(2,1)}, f32[7,400]{1,0:T(8,128)}) custom-call(bf16[35,4,1024]{2,1,0:T(4,128)(2,1)S(1)} %get-tuple-element.6.image, f32[7,400]{1,0:T(8,128)S(1)} %get-tuple-element.7.modal), custom_call_target="tpu_custom_call" | custom-call | tf_op jit(solution)/shard_map/pallas_call | solution.py:491

commit v4 on v3

--- a/solution.py
+++ b/solution.py
@@ -147,7 +147,8 @@
     def peer(i, j):
         return {"circ": lax.rem(me_circ + i, n_circ), "cell": lax.rem(me_cell + j, n_cell)}
 
-    peers = [(i, j) for i in range(n_circ) for j in range(n_cell) if i or j]
+    peers = [(i % n_circ, j) for i in range(1, n_circ + 1) for j in range(n_cell)][:-n_cell]
+    peers += [(0, j) for j in range(1, n_cell)]
     loads = {}
 
     def fetch(which):
@@ -156,11 +157,12 @@
             loads[at].start()
 
     fetch(LOAD_ORDER[:2])
-    peers = [(i, j) for i in range(n_circ) for j in range(n_cell) if i or j]
+    peers = [(i % n_circ, j) for i in range(1, n_circ + 1) for j in range(n_cell)][:-n_cell]
+    peers += [(0, j) for j in range(1, n_cell)]
     barrier = pltpu.get_barrier_semaphore()
     for i, j in peers:
         pl.semaphore_signal(barrier, inc=1, device_id=peer(i, j), device_id_type=MESH)
-    fetch(LOAD_ORDER[2:])
+    fetch(LOAD_ORDER[2:5])
 
     def load(*which):
         for at in which:
@@ -253,14 +255,21 @@
         tile = jnp.where(lane == k * 8, force, tile)
     forces[me] = jnp.sum(tile, axis=0, keepdims=True)
 
-    late = me_circ >= n_circ // 2
+    early = me_circ < n_circ // 4
+    late = me_circ >= n_circ - n_circ // 4
+    middle = jnp.logical_not(jnp.logical_or(early, late))
 
     def enter_and_send_forces():
         pl.semaphore_wait(barrier, n_cell * n_circ - 1)
         for i, j in peers:
             remote(forces.at[me], forces.at[me], force_send, force_recv, peer(i, j)).start()
 
+    def enter_and_send_all():
+        enter_and_send_forces()
+        send_sides()
+
     pl.when(late)(enter_and_send_forces)
+    fetch(LOAD_ORDER[5:])
 
     load(FACE_MAP, SIDES, PERIODIC_DAMP, AXIAL_DAMP, PICK_C)
     order = face_map[...]
@@ -321,6 +330,8 @@
         if at + part < n_faces:
             build(at + part, part)
         gather(at, part)
+        if at == starts[len(starts) // 2 - 1]:
+            pl.when(middle)(enter_and_send_all)
 
     load(MODE_SHAPES, MODES_C)
     shapes = mode_shapes[...].reshape(2 * walls_k * n_circ, mode_shapes.shape[3])
@@ -341,10 +352,7 @@
         flux[...], signed[...], NT, preferred_element_type=F32
     )
 
-    @pl.when(jnp.logical_not(late))
-    def _():
-        enter_and_send_forces()
-        send_sides()
+    pl.when(early)(enter_and_send_all)
 
     to_below.wait_recv()
     to_above.wait_recv()

time: 14.2 us -> 15.2 us (1.070)
  Pallas kernels: 13.3 us -> 14.4 us
    pallas_call x1, Pallas kernels: 12.6 us -> 13.7 us  [shards(): pl.pallas_call(functools.partial(kernel, n_in=len(operands), n_cell=n_cel...]
where the time goes in v4:
time: 15.2 us; the launch traced here: 15.1 us
  Pallas kernels  14.4 us (95%)
  between operations  0.64 us (4%)
    pallas_call x1, Pallas kernels, shards(): pl.pallas_call(functools.partial(kernel, n_in=len(operands), n_cell=n_cel...  13.7 us
    pallas_call x1, Pallas kernels, shards(): pl.pallas_call(deliver, out_shape=(jax.ShapeDtypeStruct(image.shape, BF16...  0.73 us

profile of v4, /device:TPU:0, one launch (start us, length us, event | category | flops | bytes accessed | tf_op | source)
XLA Modules:
  0.0 15.1 jit_solution(10603590227613810783)
XLA Ops:
  0.6 13.7 %shard_map.212 = (bf16[35,4,1024]{2,1,0:T(4,128)(2,1)S(1)}, f32[7,400]{1,0:T(8,128)S(1)}) custom-call(bf16[35,4,1024]{2,1,0:T(4,128)(2,1)} %bitcast.8, f32[1,4,1024]{2,1,0:T(4,128)} %refs_1_.1, bf16[1,4,1024]{2,1,0:T(4,128)(2,1)} %refs_2_.1, bf16[1,4,2048]{2,1,0:T(4,128)(2,1)} %refs_3_.1, bf16[1,4,64]{2,1,0:T(4,128)(2,1)} %refs_4_.1, f32[5,3,5]{2,1,0:T(4,128)} %bitcast.10, ...), custom_call_target="tpu_custom_call" | custom-call | tf_op jit(solution)/shard_map/pallas_call | solution.py:465
  14.3 0.7 %shard_map.213 = (bf16[35,4,1024]{2,1,0:T(4,128)(2,1)}, f32[7,400]{1,0:T(8,128)}) custom-call(bf16[35,4,1024]{2,1,0:T(4,128)(2,1)S(1)} %get-tuple-element.6.image, f32[7,400]{1,0:T(8,128)S(1)} %get-tuple-element.7.modal), custom_call_target="tpu_custom_call" | custom-call | tf_op jit(solution)/shard_map/pallas_call | solution.py:499

commit v5 on v4

--- a/solution.py
+++ b/solution.py
@@ -162,7 +162,7 @@
     barrier = pltpu.get_barrier_semaphore()
     for i, j in peers:
         pl.semaphore_signal(barrier, inc=1, device_id=peer(i, j), device_id_type=MESH)
-    fetch(LOAD_ORDER[2:5])
+    fetch(LOAD_ORDER[2:])
 
     def load(*which):
         for at in which:
@@ -193,16 +193,21 @@
         cell_at(n_cell - 1),
     )
     to_above = remote(
-        cell_out.at[pl.ds(side_rows, side_rows + 16)], below, cell_send.at[1], cell_recv.at[1],
+        cell_out.at[pl.ds(side_rows, side_rows)], below, cell_send.at[1], cell_recv.at[1],
         cell_at(1),
     )
-    to_prev = remote(side_out, side_next, side_send.at[0], side_recv.at[0], circ_at(n_circ - 1))
-    to_next = remote(side_out, side_prev, side_send.at[1], side_recv.at[1], circ_at(1))
-    copies = [to_below, to_above, to_prev, to_next]
+    to_prev = remote(
+        side_out.at[0], side_next, side_send.at[0], side_recv.at[0], circ_at(n_circ - 1)
+    )
+    to_next = remote(side_out.at[1], side_prev, side_send.at[1], side_recv.at[1], circ_at(1))
+    has_below = me_cell > 0
+    has_above = me_cell < n_cell - 1
 
     def send_sides():
-        for copy in copies:
-            copy.start()
+        to_prev.start()
+        to_next.start()
+        pl.when(has_above)(to_above.start)
+        pl.when(has_below)(to_below.start)
 
     band = lax.broadcasted_iota(jnp.int32, (GROUP, 128), 0).astype(F32).astype(BF16)
     one = jnp.ones((GROUP, 128), BF16)
@@ -269,7 +274,6 @@
         send_sides()
 
     pl.when(late)(enter_and_send_forces)
-    fetch(LOAD_ORDER[5:])
 
     load(FACE_MAP, SIDES, PERIODIC_DAMP, AXIAL_DAMP, PICK_C)
     order = face_map[...]
@@ -278,15 +282,26 @@
     targets = (targets + 0.5).astype(jnp.int32)
     mark(jnp.concatenate([sides[1:2, :], targets], axis=1), n_walls)
 
-    cell_out[0 : 2 * side_rows, :] = dot(pick_c[...], u).astype(BF16)
+    own_side = dot(u, extra[:, n_walls:])
+    side_damp = periodic_damp[0].astype(F32)
+    side_pattern = pattern_of(jnp.concatenate([side_damp, side_damp], axis=1))
+    half = padded // 2
+    left = lax.broadcasted_iota(jnp.int32, (half, 2 * per), 1) < per
+    first_half, second_half = own_side[0:half], own_side[half:]
+    filler = [side_pattern] * ((side_out.shape[1] - half) // 8)
+    lower_own = jnp.where(left, pltpu.roll(first_half, per, 1), second_half)
+    upper_own = jnp.where(left, first_half, pltpu.roll(second_half, per, 1))
+    side_out[0] = jnp.concatenate([lower_own, *filler], axis=0).astype(BF16)
+    side_out[1] = jnp.concatenate([upper_own, *filler], axis=0).astype(BF16)
+
     damp = axial_damp[0].astype(F32)
     last = damp[layers - 1 : layers]
-    cell_out[2 * side_rows :, :] = jnp.broadcast_to(last, (16, cells)).astype(BF16)
-    own_side = dot(u, extra[:, n_walls:])
-    side_out[0:padded, :] = own_side.astype(BF16)
-    side_damp = periodic_damp[0].astype(F32)
-    side_pattern = pattern_of(jnp.concatenate([side_damp, side_damp], axis=1))
-    side_out[padded:, :] = jnp.concatenate([side_pattern, side_pattern], axis=0).astype(BF16)
+    picked = dot(pick_c[...], u)
+    spare = lax.broadcasted_iota(jnp.int32, (16, cells), 0) == 15
+    tail = jnp.where(spare, jnp.broadcast_to(last, (16, cells)), picked[2 * side_rows - 16 :])
+    cell_out[0 : 2 * side_rows - 16, :] = picked[0 : 2 * side_rows - 16].astype(BF16)
+    cell_out[2 * side_rows - 16 :, :] = tail.astype(BF16)
+
     pl.when(late)(send_sides)
 
     load(JAC, OF_ROW_C, OF_COLUMN_C, MIX_C, AXIAL_C, PLANE_DAMP, FACES)
@@ -354,18 +369,18 @@
 
     pl.when(early)(enter_and_send_all)
 
-    to_below.wait_recv()
-    to_above.wait_recv()
+    pl.when(has_above)(to_below.wait_recv)
+    pl.when(has_below)(to_above.wait_recv)
     load(FIXED_C, TIME_COEF)
     above_rows = above[...].astype(F32)
     stack[padded : padded + side_rows, :] = jnp.where(
         me_cell == n_cell - 1, 0.0, above_rows
     ).astype(BF16)
-    below_rows = below[0:side_rows, :].astype(F32)
+    below_rows = below[...].astype(F32)
     stack[padded + side_rows :, :] = jnp.where(
         me_cell == 0, -cell_out[0:side_rows, :].astype(F32), below_rows
     ).astype(BF16)
-    below_damp = below[side_rows : side_rows + 16, :].astype(F32)[0:1]
+    below_damp = below[side_rows - 16 : side_rows, :].astype(F32)[15:16]
     below_damp = jnp.where(me_cell == 0, 0.0, below_damp)
     held = stack[...]
     derived = dot(fixed_c[...], held)
@@ -377,10 +392,12 @@
 
     to_prev.wait_recv()
     to_next.wait_recv()
-    left = lax.broadcasted_iota(jnp.int32, (padded, 2 * per), 1) < per
-    ahead = pltpu.roll(side_next[0:padded, :].astype(F32), per, 1)
-    back = pltpu.roll(side_prev[0:padded, :].astype(F32), per, 1)
-    back_damp = side_prev[padded:, :].astype(F32)[0:8]
+    ahead = side_next[0:half, :].astype(F32)
+    back = side_prev[0:half, :].astype(F32)
+    back_damp = side_prev[half:, :].astype(F32)[0:8]
+    ahead = jnp.concatenate([ahead, pltpu.roll(ahead, per, 1)], axis=0)
+    back = jnp.concatenate([pltpu.roll(back, per, 1), back], axis=0)
+    left = jnp.concatenate([left, left], axis=0)
     lower = jnp.where(left, own_side, back)
     upper = jnp.where(left, ahead, own_side)
     side_s = 0.5 * jnp.where(left[0:8], side_pattern, back_damp)
@@ -417,8 +434,10 @@
     answer = dot(high, table) + dot(low, table) + dot(high, modes_low[...])
     modal[...] = answer[0:HB]
     arrived.wait_send()
-    for copy in copies:
-        copy.wait_send()
+    to_prev.wait_send()
+    to_next.wait_send()
+    pl.when(has_above)(to_above.wait_send)
+    pl.when(has_below)(to_below.wait_send)
 
 
 def deliver(image, modal, image_out, modal_out, sems):
@@ -448,6 +467,7 @@
     padded = fixed[0].shape[0]
     side = fixed[3].shape[0] // 2
     lanes = force_slots(n_circ, walls_k)[2]
+    packed = up_to(padded // 2 + 8, 16)
     state = flow_state.reshape(HB * NV, layers, cells)
     vmem = pl.BlockSpec(memory_space=pltpu.VMEM)
     dma = pltpu.SemaphoreType.DMA
@@ -479,12 +499,12 @@
             pltpu.VMEM((cells, n_faces), F8),
             pltpu.VMEM((cells, n_faces), F8),
             pltpu.VMEM((padded + 2 * side, cells), BF16),
-            pltpu.VMEM((2 * side + 16, cells), BF16),
+            pltpu.VMEM((2 * side, cells), BF16),
             pltpu.VMEM((side, cells), BF16),
-            pltpu.VMEM((side + 16, cells), BF16),
-            pltpu.VMEM((padded + 16, 2 * per), BF16),
-            pltpu.VMEM((padded + 16, 2 * per), BF16),
-            pltpu.VMEM((padded + 16, 2 * per), BF16),
+            pltpu.VMEM((side, cells), BF16),
+            pltpu.VMEM((2, packed, 2 * per), BF16),
+            pltpu.VMEM((packed, 2 * per), BF16),
+            pltpu.VMEM((packed, 2 * per), BF16),
             pltpu.VMEM((n_circ * n_cell, 1, 128), F32),
             pltpu.VMEM((lanes, n_modes), BF16),
             pltpu.VMEM((lanes, n_modes), BF16),

time: 15.2 us -> 13.7 us (0.901)
  the two profiles are of different devices: /device:TPU:0 before, /device:TPU:1 now
where the time goes in v5:
time: 13.7 us; the launch traced here: 13.6 us
  Pallas kernels  13 us (95%)
  between operations  0.64 us (5%)
    pallas_call x1, Pallas kernels, shards(): pl.pallas_call(functools.partial(kernel, n_in=len(operands), n_cell=n_cel...  12.2 us
    pallas_call x1, Pallas kernels, shards(): pl.pallas_call(deliver, out_shape=(jax.ShapeDtypeStruct(image.shape, BF16...  0.73 us

profile of v5, /device:TPU:1, one launch (start us, length us, event | category | flops | bytes accessed | tf_op | source)
XLA Modules:
  0.0 13.6 jit_solution(10682814590334341303)
XLA Ops:
  0.6 12.2 %shard_map.212 = (bf16[35,4,1024]{2,1,0:T(4,128)(2,1)S(1)}, f32[7,400]{1,0:T(8,128)S(1)}) custom-call(bf16[35,4,1024]{2,1,0:T(4,128)(2,1)} %bitcast.8, f32[1,4,1024]{2,1,0:T(4,128)} %refs_1_.1, bf16[1,4,1024]{2,1,0:T(4,128)(2,1)} %refs_2_.1, bf16[1,4,2048]{2,1,0:T(4,128)(2,1)} %refs_3_.1, bf16[1,4,64]{2,1,0:T(4,128)(2,1)} %refs_4_.1, f32[5,3,5]{2,1,0:T(4,128)} %bitcast.10, ...), custom_call_target="tpu_custom_call" | custom-call | tf_op jit(solution)/shard_map/pallas_call | solution.py:485
  12.9 0.7 %shard_map.213 = (bf16[35,4,1024]{2,1,0:T(4,128)(2,1)}, f32[7,400]{1,0:T(8,128)}) custom-call(bf16[35,4,1024]{2,1,0:T(4,128)(2,1)S(1)} %get-tuple-element.6.image, f32[7,400]{1,0:T(8,128)S(1)} %get-tuple-element.7.modal), custom_call_target="tpu_custom_call" | custom-call | tf_op jit(solution)/shard_map/pallas_call | solution.py:519

commit v6 on v5

--- a/solution.py
+++ b/solution.py
@@ -204,10 +204,10 @@
     has_above = me_cell < n_cell - 1
 
     def send_sides():
+        pl.when(has_above)(to_above.start)
+        pl.when(has_below)(to_below.start)
         to_prev.start()
         to_next.start()
-        pl.when(has_above)(to_above.start)
-        pl.when(has_below)(to_below.start)
 
     band = lax.broadcasted_iota(jnp.int32, (GROUP, 128), 0).astype(F32).astype(BF16)
     one = jnp.ones((GROUP, 128), BF16)
@@ -261,17 +261,23 @@
     forces[me] = jnp.sum(tile, axis=0, keepdims=True)
 
     early = me_circ < n_circ // 4
-    late = me_circ >= n_circ - n_circ // 4
-    middle = jnp.logical_not(jnp.logical_or(early, late))
-
-    def enter_and_send_forces():
+    late = me_circ >= n_circ // 4
+
+    def enter():
         pl.semaphore_wait(barrier, n_cell * n_circ - 1)
+
+    def send_forces():
         for i, j in peers:
             remote(forces.at[me], forces.at[me], force_send, force_recv, peer(i, j)).start()
 
+    def enter_and_send_forces():
+        enter()
+        send_forces()
+
     def enter_and_send_all():
-        enter_and_send_forces()
+        enter()
         send_sides()
+        send_forces()
 
     pl.when(late)(enter_and_send_forces)
 
@@ -345,8 +351,6 @@
         if at + part < n_faces:
             build(at + part, part)
         gather(at, part)
-        if at == starts[len(starts) // 2 - 1]:
-            pl.when(middle)(enter_and_send_all)
 
     load(MODE_SHAPES, MODES_C)
     shapes = mode_shapes[...].reshape(2 * walls_k * n_circ, mode_shapes.shape[3])
@@ -363,11 +367,12 @@
         modes_high[first : first + pitch, :] = high
         modes_low[first : first + pitch, :] = (rows - high.astype(F32)).astype(BF16)
 
+    pl.when(early)(enter_and_send_all)
+
     total[...] = lax.dot_general(
         flux[...], signed[...], NT, preferred_element_type=F32
     )
 
-    pl.when(early)(enter_and_send_all)
 
     pl.when(has_above)(to_below.wait_recv)
     pl.when(has_below)(to_above.wait_recv)

time: 13.7 us -> 12.9 us (0.942)
  the two profiles are of different devices: /device:TPU:1 before, /device:TPU:0 now
where the time goes in v6:
time: 12.9 us; the launch traced here: 12.7 us
  Pallas kernels  12.1 us (94%)
  between operations  0.64 us (5%)
    pallas_call x1, Pallas kernels, shards(): pl.pallas_call(functools.partial(kernel, n_in=len(operands), n_cell=n_cel...  11.3 us
    pallas_call x1, Pallas kernels, shards(): pl.pallas_call(deliver, out_shape=(jax.ShapeDtypeStruct(image.shape, BF16...  0.73 us

profile of v6, /device:TPU:0, one launch (start us, length us, event | category | flops | bytes accessed | tf_op | source)
XLA Modules:
  0.0 12.7 jit_solution(8918125882981465178)
XLA Ops:
  0.6 11.3 %shard_map.212 = (bf16[35,4,1024]{2,1,0:T(4,128)(2,1)S(1)}, f32[7,400]{1,0:T(8,128)S(1)}) custom-call(bf16[35,4,1024]{2,1,0:T(4,128)(2,1)} %bitcast.8, f32[1,4,1024]{2,1,0:T(4,128)} %refs_1_.1, bf16[1,4,1024]{2,1,0:T(4,128)(2,1)} %refs_2_.1, bf16[1,4,2048]{2,1,0:T(4,128)(2,1)} %refs_3_.1, bf16[1,4,64]{2,1,0:T(4,128)(2,1)} %refs_4_.1, f32[5,3,5]{2,1,0:T(4,128)} %bitcast.10, ...), custom_call_target="tpu_custom_call" | custom-call | tf_op jit(solution)/shard_map/pallas_call | solution.py:490
  12.0 0.7 %shard_map.213 = (bf16[35,4,1024]{2,1,0:T(4,128)(2,1)}, f32[7,400]{1,0:T(8,128)}) custom-call(bf16[35,4,1024]{2,1,0:T(4,128)(2,1)S(1)} %get-tuple-element.6.image, f32[7,400]{1,0:T(8,128)S(1)} %get-tuple-element.7.modal), custom_call_target="tpu_custom_call" | custom-call | tf_op jit(solution)/shard_map/pallas_call | solution.py:524
